TPU v7x, 32 devices: a whole 2x2x4 slice. The times are simulated.
32 devices in a mesh: img: 8 (over z, core), pix: 4 (over y, x).
Axes of the slice: x: 2, y: 2, z: 4, core: 2. Of those that a mesh axis runs over, the one named last changes fastest.
Arguments:
- images: bfloat16 [25600, 16384], P('img', 'pix'), may hold values from -6 to 6
- classes: int32 [25600], P('img'), may hold values from 0 to 63
- ctf_table: bfloat16 [64, 16384], P(None, 'pix'), may hold values from -1 to 1, as said below
- weights: float32 [25600], P('img'), may hold values from 0.1 to 1
- probes: float32 [16384, 256], P('pix'), may hold values from -6 to 6
Outputs:
- basis: float32 [16384, 256], P('pix')
- factor: float32 [256, 256], replicated
Inputs may be any that keep to these rules, and one draw needn't show every extreme that they name: `ctf_table`: a smooth envelope over the pixel index times an independent magnitude and sign for each entry.
All inputs are finite; a program needn't handle non-finite values.
Results may differ from a plain program's by a relative error of at most 0.012.
Values may be sent and summed in bfloat16 or wider, within the bound.
No kernel may reach another device: no remote copies, remote signals or barrier semaphores. Data moves between devices by JAX's collectives and lax.ppermute only.
A program may use at most 128 MiB of HBM per device.

v0:
```python
import jax
import jax.numpy as jnp
from jax import lax
from jax.sharding import PartitionSpec as P

ITERS = 2


def per_device(images, classes, ctf_table, weights, probes):
    onehot = (classes[:, None] == jnp.arange(ctf_table.shape[0])[None, :]).astype(jnp.bfloat16)
    filters = jnp.dot(onehot, ctf_table, preferred_element_type=jnp.float32)
    filtered = (images.astype(jnp.float32) * filters).astype(jnp.bfloat16)
    current = probes
    factor = jnp.zeros((probes.shape[1], probes.shape[1]), jnp.float32)
    for sweep in range(ITERS):
        probe_half = current.astype(jnp.bfloat16)
        share_rows = filtered.shape[0] // lax.axis_size("pix")
        shares = lax.psum_scatter(
            jnp.dot(filtered, probe_half, preferred_element_type=jnp.float32),
            "pix",
            scatter_dimension=0,
            tiled=True,
        )
        weight_share = lax.dynamic_slice_in_dim(
            weights, lax.axis_index("pix") * share_rows, share_rows, 0
        )
        scaled_share = (weight_share[:, None] * shares).astype(jnp.bfloat16)
        scaled = lax.all_gather(scaled_share, "pix", axis=0, tiled=True)
        partial_sum = lax.dot_general(
            filtered, scaled, (((0,), (0,)), ((), ())), preferred_element_type=jnp.float32
        )
        image_sum = lax.psum(partial_sum, "img")
        gram_matrix = lax.psum(
            jnp.dot(image_sum.T, image_sum, precision=lax.Precision.HIGHEST), "pix"
        )
        factor = jnp.linalg.cholesky(gram_matrix)
        current = jax.scipy.linalg.solve_triangular(factor, image_sum.T, lower=True).T
    return (current, factor)


def solution(mesh):
    in_specs = (P("img", "pix"), P("img"), P(None, "pix"), P("img"), P("pix", None))
    out_specs = (P("pix", None), P())
    return jax.shard_map(
        per_device, mesh=mesh, in_specs=in_specs, out_specs=out_specs, check_vma=False
    )
```

profile of v0, /device:TPU:0, one launch (start us, length us, event | category | flops | bytes accessed | tf_op | source)
XLA Modules:
  0.0 707.9 jit_solution(17062650772016324928)
XLA Ops:
  7.2 1.0 copy-done
  8.2 21.5 %multiply_convert_fusion = bf16[3200,4096]{1,0:T(8,128)(2,1)} fusion(bf16[3200,4096]{1,0:T(8,128)(2,1)} %param.8, bf16[64,4096]{1,0:T(8,128)(2,1)S(1)} %copy-done, s32[3200]{0:T(1024)} %param.9), kind=kOutput, calls=%fused_computation.4 | convolution fusion | flops 1717248000 | bytes 52965888 | tf_op jit(solution)/shard_map/dot_general | solution.py:11
  29.7 14.4 %fusion.5 = f32[3200,256]{1,0:T(8,128)} fusion(bf16[3200,4096]{1,0:T(8,128)(2,1)} %multiply_convert_fusion, f32[4096,256]{1,0:T(8,128)} %param.12), kind=kOutput, calls=%fused_computation.14 | convolution fusion | flops 6711934976 | bytes 33685504 | tf_op jit(solution)/shard_map/dot_general | solution.py:19
  44.2 0.8 dynamic_slice.4
  45.0 47.0 %reduce-scatter.3.cloned.1.call-done = f32[800,256]{1,0:T(8,128)} async-done(((f32[3200,256]{1,0:T(8,128)}), f32[800,256]{1,0:T(8,128)}) %reduce-scatter.3.cloned.1.call-update) | async-done | bytes 819216 | tf_op jit(solution)/shard_map/reduce_scatter | solution.py:18
  92.0 2.1 multiply_convert_fusion.2
  94.1 0.0 all-reduce.6.cloned.1.call-start
  94.2 31.7 %all-gather.3.cloned.1.call-done = bf16[3200,256]{1,0:T(8,128)(2,1)} async-done(((bf16[800,256]{1,0:T(8,128)(2,1)}), bf16[3200,256]{1,0:T(8,128)(2,1)}) %all-gather.3.cloned.1.call-update) | async-done | bytes 1638416 | tf_op jit(solution)/shard_map/all_gather | solution.py:28
  125.9 14.4 %fusion.30 = f32[4096,256]{1,0:T(8,128)} fusion(bf16[3200,4096]{1,0:T(8,128)(2,1)} %multiply_convert_fusion, bf16[3200,256]{1,0:T(8,128)(2,1)} %all-gather.3.cloned.1.call-done), kind=kOutput, calls=%fused_computation.66 | convolution fusion | flops 6710886400 | bytes 32047104 | tf_op jit(solution)/shard_map/dot_general | solution.py:29
  140.3 0.5 all-reduce.8.cloned.1.call-start
  140.8 96.1 %all-reduce.6.cloned.1.call-done = f32[4096,256]{1,0:T(8,128)} async-done(((f32[4096,256]{1,0:T(8,128)}), f32[4096,256]{1,0:T(8,128)}) %all-reduce.6.cloned.1.call-update) | async-done | bytes 4194320 | tf_op jit(solution)/shard_map/psum | solution.py:32
  236.9 10.9 %fusion.31 = f32[256,256]{0,1:T(8,128)} fusion(f32[4096,256]{1,0:T(8,128)} %all-reduce.6.cloned.1.call-done), kind=kOutput, calls=%fused_computation.67 | convolution fusion | flops 3221225472 | bytes 4456448 | tf_op jit(solution)/shard_map/dot_general | solution.py:34
  247.9 0.2 reduce-scatter.5.cloned.1.call-start
  248.1 43.0 %all-reduce.8.cloned.1.call-done = f32[256,256]{0,1:T(8,128)} async-done(((f32[256,256]{0,1:T(8,128)}), f32[256,256]{0,1:T(8,128)}) %all-reduce.8.cloned.1.call-update) | async-done | bytes 262160 | tf_op jit(solution)/shard_map/psum | solution.py:33
  291.1 1.1 copy.8
  292.2 1.0 fusion.9
  293.2 11.7 %cholesky.130 = f32[128,128]{1,0:T(8,128)S(1)} custom-call(f32[128,128]{1,0:T(8,128)S(1)} %cholesky.194), custom_call_target="Cholesky" | custom-call | tf_op jit(solution)/shard_map/jit(cholesky)/cholesky | solution.py:36
  305.0 9.8 %custom-call.13 = f32[1,128,128]{1,2,0:T(8,128)S(1)} custom-call(f32[1,128,128]{2,1,0:T(8,128)S(1)} %get-tuple-element.51), custom_call_target="InvertDiagBlocksLowerTriangular" | custom-call | tf_op jit(solution)/shard_map/jit(cholesky)/cholesky | solution.py:36
  314.8 0.2 constant_dynamic-update-slice_fusion.3
  315.0 0.3 convolution_subtract_fusion.3
  315.3 11.7 %cholesky.147 = f32[128,128]{1,0:T(8,128)S(1)} custom-call(f32[128,128]{1,0:T(8,128)S(1)} %convolution_subtract_fusion.3), custom_call_target="Cholesky" | custom-call | tf_op jit(solution)/shard_map/jit(cholesky)/cholesky | solution.py:36
  327.0 0.7 compare_reduce_fusion.2
  329.0 0.1 triangular_solve.75
  329.1 4.2 while.4
  329.3 0.6 fusion.55
  329.9 1.4 bitcast_dynamic-update-slice_fusion.4
  331.3 0.6 fusion.55
  331.9 1.4 bitcast_dynamic-update-slice_fusion.4
  333.3 19.7 %custom-call.14 = f32[2,128,128]{1,2,0:T(8,128)S(1)} custom-call(f32[2,128,128]{2,1,0:T(8,128)S(1)} %get-tuple-element.18), custom_call_target="InvertDiagBlocksLowerTriangular" | custom-call | tf_op jit(solution)/shard_map/jit(_solve_triangular)/triangular_solve | solution.py:37
  353.0 3.7 fusion.3
  356.7 3.6 convolution_subtract_fusion.1
  360.3 1.9 fusion.17
  362.2 14.2 %fusion = f32[3200,256]{1,0:T(8,128)} fusion(bf16[3200,4096]{1,0:T(8,128)(2,1)} %multiply_convert_fusion, bf16[128,4096]{1,0:T(8,128)(2,1)S(1)} %fusion.17, f32[128,4096]{1,0:T(8,128)S(1)} %fusion.3), kind=kOutput, calls=%fused_computation.9 | convolution fusion | flops 6715080704 | bytes 32636928 | tf_op jit(solution)/shard_map/dot_general | solution.py:19
  376.4 0.0 all-gather.5.cloned.1.call-start
  376.5 45.1 %reduce-scatter.5.cloned.1.call-done = f32[800,256]{1,0:T(8,128)} async-done(((f32[3200,256]{1,0:T(8,128)}), f32[800,256]{1,0:T(8,128)}) %reduce-scatter.5.cloned.1.call-update) | async-done | bytes 819216 | tf_op jit(solution)/shard_map/reduce_scatter | solution.py:18
  421.6 2.1 multiply_convert_fusion.1
  423.7 0.0 all-reduce.10.cloned.1.call-start
  423.7 31.5 %all-gather.5.cloned.1.call-done = bf16[3200,256]{1,0:T(8,128)(2,1)} async-done(((bf16[800,256]{1,0:T(8,128)(2,1)}), bf16[3200,256]{1,0:T(8,128)(2,1)}) %all-gather.5.cloned.1.call-update) | async-done | bytes 1638416 | tf_op jit(solution)/shard_map/all_gather | solution.py:28
  455.3 14.4 %fusion.32 = f32[4096,256]{1,0:T(8,128)} fusion(bf16[3200,4096]{1,0:T(8,128)(2,1)} %multiply_convert_fusion, bf16[3200,256]{1,0:T(8,128)(2,1)} %all-gather.5.cloned.1.call-done), kind=kOutput, calls=%fused_computation.68 | convolution fusion | flops 6710886400 | bytes 32047104 | tf_op jit(solution)/shard_map/dot_general | solution.py:29
  469.7 0.2 all-reduce.12.cloned.1.call-start
  469.9 96.4 %all-reduce.10.cloned.1.call-done = f32[4096,256]{1,0:T(8,128)} async-done(((f32[4096,256]{1,0:T(8,128)}), f32[4096,256]{1,0:T(8,128)}) %all-reduce.10.cloned.1.call-update) | async-done | bytes 4194320 | tf_op jit(solution)/shard_map/psum | solution.py:32
  566.3 10.9 %fusion.33 = f32[256,256]{0,1:T(8,128)} fusion(f32[4096,256]{1,0:T(8,128)} %all-reduce.10.cloned.1.call-done), kind=kOutput, calls=%fused_computation.69 | convolution fusion | flops 3221225472 | bytes 4456448 | tf_op jit(solution)/shard_map/dot_general | solution.py:34
  577.3 43.2 %all-reduce.12.cloned.1.call-done = f32[256,256]{0,1:T(8,128)} async-done(((f32[256,256]{0,1:T(8,128)}), f32[256,256]{0,1:T(8,128)}) %all-reduce.12.cloned.1.call-update) | async-done | bytes 262160 | tf_op jit(solution)/shard_map/psum | solution.py:33
  620.5 1.1 copy.10
  621.6 1.0 fusion.8
  622.6 11.7 %cholesky.164 = f32[128,128]{1,0:T(8,128)S(1)} custom-call(f32[128,128]{1,0:T(8,128)S(1)} %cholesky.197), custom_call_target="Cholesky" | custom-call | tf_op jit(solution)/shard_map/jit(cholesky)/cholesky | solution.py:36
  634.4 10.0 %custom-call.15 = f32[1,128,128]{1,2,0:T(8,128)S(1)} custom-call(f32[1,128,128]{2,1,0:T(8,128)S(1)} %get-tuple-element.47), custom_call_target="InvertDiagBlocksLowerTriangular" | custom-call | tf_op jit(solution)/shard_map/jit(cholesky)/cholesky | solution.py:36
  644.4 0.2 constant_dynamic-update-slice_fusion.1
  644.6 0.3 convolution_subtract_fusion.2
  644.9 11.7 %cholesky.181 = f32[128,128]{1,0:T(8,128)S(1)} custom-call(f32[128,128]{1,0:T(8,128)S(1)} %convolution_subtract_fusion.2), custom_call_target="Cholesky" | custom-call | tf_op jit(solution)/shard_map/jit(cholesky)/cholesky | solution.py:36
  656.6 0.6 compare_reduce_fusion
  657.2 0.6 compare_reduce_fusion.1
  659.2 0.7 fusion.11
  659.9 3.9 while.5
  660.0 0.6 fusion.56
  660.5 1.4 bitcast_dynamic-update-slice_fusion.5
  661.9 0.6 fusion.56
  662.5 1.4 bitcast_dynamic-update-slice_fusion.5
  663.9 19.7 %custom-call.16 = f32[2,128,128]{1,2,0:T(8,128)S(1)} custom-call(f32[2,128,128]{2,1,0:T(8,128)S(1)} %get-tuple-element.19), custom_call_target="InvertDiagBlocksLowerTriangular" | custom-call | tf_op jit(solution)/shard_map/jit(_solve_triangular)/triangular_solve | solution.py:37
  683.6 3.7 fusion.1
  687.3 3.4 convolution_subtract_fusion
  690.7 2.0 fusion.13
  692.7 2.4 maximum_bitcast_fusion
  695.1 5.6 copy.11
  (33 shorter events, 0.5 us)
Async XLA Ops:
  7.2 1.1 copy-start
  7.2 84.8 %reduce-scatter.3.cloned.1.call-start = ((), (), s32[]{:S(2)}) async-start(), calls=%async_computation.2 | async-start | bytes 4096000 | tf_op jit(solution)/shard_map/reduce_scatter | solution.py:18
  44.1 81.7 %all-gather.3.cloned.1.call-start = ((), (), s32[]{:S(2)}) async-start(), calls=%async_computation.3 | async-start | bytes 2048000 | tf_op jit(solution)/shard_map/all_gather | solution.py:28
  94.1 142.8 %all-reduce.6.cloned.1.call-start = ((), (), s32[]{:S(2)}) async-start(), calls=%async_computation.4 | async-start | bytes 8388608 | tf_op jit(solution)/shard_map/psum | solution.py:32
  140.3 150.8 %all-reduce.8.cloned.1.call-start = ((), (), s32[]{:S(2)}) async-start(), calls=%async_computation.5 | async-start | bytes 524288 | tf_op jit(solution)/shard_map/psum | solution.py:33
  247.9 173.7 %reduce-scatter.5.cloned.1.call-start = ((), (), s32[]{:S(2)}) async-start(), calls=%async_computation.6 | async-start | bytes 4096000 | tf_op jit(solution)/shard_map/reduce_scatter | solution.py:18
  353.0 3.7 copy-start.2
  376.4 78.8 %all-gather.5.cloned.1.call-start = ((), (), s32[]{:S(2)}) async-start(), calls=%async_computation.7 | async-start | bytes 2048000 | tf_op jit(solution)/shard_map/all_gather | solution.py:28
  423.7 142.6 %all-reduce.10.cloned.1.call-start = ((), (), s32[]{:S(2)}) async-start(), calls=%async_computation.8 | async-start | bytes 8388608 | tf_op jit(solution)/shard_map/psum | solution.py:32
  469.7 150.8 %all-reduce.12.cloned.1.call-start = ((), (), s32[]{:S(2)}) async-start(), calls=%async_computation.9 | async-start | bytes 524288 | tf_op jit(solution)/shard_map/psum | solution.py:33
  683.6 3.7 copy-start.3
  692.7 8.0 %copy-start.1 = (bf16[64,4096]{1,0:T(8,128)(2,1)S(1)}, bf16[64,4096]{1,0:T(8,128)(2,1)}, u32[]{:S(2)}) copy-start(bf16[64,4096]{1,0:T(8,128)(2,1)} %param.10) | copy-start | bytes 1572868
Sparse Core Ops, SparseCore 0:
  44.3 47.7 reduce-scatter.2
  94.4 31.3 all-gather.2
  140.4 96.4 all-reduce.5
  248.0 43.0 all-reduce.7
  376.6 44.9 reduce-scatter.4
  423.9 31.3 all-gather.4
  469.8 96.4 all-reduce.9
  577.4 43.0 all-reduce.11
where the time goes:
time: 716 us; the launch traced here: 708 us
  waiting for transfers between devices  434 us (61%)
  matrix products  120 us (17%)
  other arithmetic  117 us (16%)
  local copies, waits for them, and re-layouts  17.5 us (2%)
  between operations  17.3 us (2%)
    psum x2, waiting for transfers between devices, per_device(): image_sum = lax.psum(partial_sum, 'img')  193 us
    reduce_scatter x2, waiting for transfers between devices, per_device(): lax.psum_scatter(jnp.dot(filtered, probe_half, preferred_element_type=jnp...  92.2 us
    psum x2, waiting for transfers between devices, per_device(): lax.psum(jnp.dot(image_sum.T, image_sum, precision=lax.Precision.HIGHEST)...  86.3 us
    another operation x13, other arithmetic, per_device(): factor = jnp.linalg.cholesky(gram_matrix)  68.7 us
    all_gather x2, waiting for transfers between devices, per_device(): scaled = lax.all_gather(scaled_share, 'pix', axis=0, tiled=True)  63.2 us
    another operation x5, other arithmetic, per_device(): jax.scipy.linalg.solve_triangular(factor, image_sum.T, lower=True)  40.1 us
    dot_general x2, matrix products, per_device(): lax.dot_general(filtered, scaled, (((0,), (0,)), ((), ())), preferred_ele...  28.8 us
    dot_general x2, matrix products, per_device(): jnp.dot(filtered, probe_half, preferred_element_type=jnp.float32)  28.6 us
  transfers between devices with their start and end apart: 8, of which 8 were waited for; matrix products, arithmetic and copies ran while one was open for 0% of the time, Pallas kernels for 0%

commit v1 on v0

--- a/solution.py
+++ b/solution.py
@@ -29,7 +29,8 @@
         partial_sum = lax.dot_general(
             filtered, scaled, (((0,), (0,)), ((), ())), preferred_element_type=jnp.float32
         )
-        image_sum = lax.psum(partial_sum, "img")
+        shards = lax.all_gather(partial_sum, "img", axis=0, tiled=False)
+        image_sum = shards.sum(axis=0)
         gram_matrix = lax.psum(
             jnp.dot(image_sum.T, image_sum, precision=lax.Precision.HIGHEST), "pix"
         )

time: 716 us -> 1130 us (1.58)
  waiting for transfers between devices: 434 us -> 815 us
  other arithmetic: 117 us -> 147 us
    all_gather x0 -> x2, waiting for transfers between devices: none -> 577 us  [per_device(): shards = lax.all_gather(partial_sum, 'img', axis=0, tiled=False)]
    psum x2 -> x0, waiting for transfers between devices: 193 us -> none  [per_device(): image_sum = lax.psum(partial_sum, 'img')]
    reduce_sum x0 -> x2, other arithmetic: none -> 28.8 us  [per_device(): image_sum = shards.sum(axis=0)]
where the time goes in v1:
time: 1130 us; the launch traced here: 1120 us
  waiting for transfers between devices  815 us (72%)
  other arithmetic  147 us (13%)
  matrix products  120 us (11%)
  local copies, waits for them, and re-layouts  17.8 us (2%)
  between operations  17.5 us (2%)
    all_gather x2, waiting for transfers between devices, per_device(): shards = lax.all_gather(partial_sum, 'img', axis=0, tiled=False)  577 us
    reduce_scatter x2, waiting for transfers between devices, per_device(): lax.psum_scatter(jnp.dot(filtered, probe_half, preferred_element_type=jnp...  92.1 us
    psum x2, waiting for transfers between devices, per_device(): lax.psum(jnp.dot(image_sum.T, image_sum, precision=lax.Precision.HIGHEST)...  82.5 us
    another operation x13, other arithmetic, per_device(): factor = jnp.linalg.cholesky(gram_matrix)  68.9 us
    all_gather x2, waiting for transfers between devices, per_device(): scaled = lax.all_gather(scaled_share, 'pix', axis=0, tiled=True)  63.2 us
    another operation x5, other arithmetic, per_device(): jax.scipy.linalg.solve_triangular(factor, image_sum.T, lower=True)  40.4 us
    reduce_sum x2, other arithmetic, per_device(): image_sum = shards.sum(axis=0)  28.8 us
    dot_general x2, matrix products, per_device(): lax.dot_general(filtered, scaled, (((0,), (0,)), ((), ())), preferred_ele...  28.8 us
  transfers between devices with their start and end apart: 8, of which 8 were waited for; matrix products, arithmetic and copies ran while one was open for 0% of the time, Pallas kernels for 0%

profile of v1, /device:TPU:0, one launch (start us, length us, event | category | flops | bytes accessed | tf_op | source)
XLA Modules:
  0.0 1117.9 jit_solution(2997258464826088800)
XLA Ops:
  7.2 1.0 copy-done
  8.2 21.4 %multiply_convert_fusion = bf16[3200,4096]{1,0:T(8,128)(2,1)} fusion(bf16[3200,4096]{1,0:T(8,128)(2,1)} %param.8, bf16[64,4096]{1,0:T(8,128)(2,1)S(1)} %copy-done, s32[3200]{0:T(1024)} %param.9), kind=kOutput, calls=%fused_computation.4 | convolution fusion | flops 1717248000 | bytes 52965888 | tf_op jit(solution)/shard_map/dot_general | solution.py:11
  29.7 14.4 %fusion.5 = f32[3200,256]{1,0:T(8,128)} fusion(bf16[3200,4096]{1,0:T(8,128)(2,1)} %multiply_convert_fusion, f32[4096,256]{1,0:T(8,128)} %param.12), kind=kOutput, calls=%fused_computation.14 | convolution fusion | flops 6711934976 | bytes 33685504 | tf_op jit(solution)/shard_map/dot_general | solution.py:19
  44.2 0.8 dynamic_slice.4
  44.9 47.0 %reduce-scatter.3.cloned.1.call-done = f32[800,256]{1,0:T(8,128)} async-done(((f32[3200,256]{1,0:T(8,128)}), f32[800,256]{1,0:T(8,128)}) %reduce-scatter.3.cloned.1.call-update) | async-done | bytes 819216 | tf_op jit(solution)/shard_map/reduce_scatter | solution.py:18
  92.0 2.1 multiply_convert_fusion.2
  94.1 31.7 %all-gather.7.cloned.1.call-done = bf16[3200,256]{1,0:T(8,128)(2,1)} async-done(((bf16[800,256]{1,0:T(8,128)(2,1)}), bf16[3200,256]{1,0:T(8,128)(2,1)}) %all-gather.7.cloned.1.call-update) | async-done | bytes 1638416 | tf_op jit(solution)/shard_map/all_gather | solution.py:28
  125.8 14.4 %fusion.30 = f32[4096,256]{1,0:T(8,128)} fusion(bf16[3200,4096]{1,0:T(8,128)(2,1)} %multiply_convert_fusion, bf16[3200,256]{1,0:T(8,128)(2,1)} %all-gather.7.cloned.1.call-done), kind=kOutput, calls=%fused_computation.66 | convolution fusion | flops 6710886400 | bytes 32047104 | tf_op jit(solution)/shard_map/dot_general | solution.py:29
  140.2 0.6 all-reduce.4.cloned.1.call-start
  140.8 288.2 %all-gather.11.cloned.1.call-done = f32[32768,256]{1,0:T(8,128)} async-done(((f32[4096,256]{1,0:T(8,128)}), f32[32768,256]{1,0:T(8,128)}) %all-gather.11.cloned.1.call-update) | async-done | bytes 33554448 | tf_op jit(solution)/shard_map/all_gather | solution.py:32
  429.0 14.3 %reduce_sum.18 = f32[4096,256]{1,0:T(8,128)} reduce(f32[8,4096,256]{2,1,0:T(8,128)} %bitcast.83, f32[]{:T(128)} %constant.69.clone.1), dimensions={0}, to_apply=%region_1.0 | reduce | flops 7340032 | bytes 37748740 | tf_op jit(solution)/shard_map/reduce_sum | solution.py:33
  443.3 10.9 fusion.31
  454.2 0.2 reduce-scatter.5.cloned.1.call-start
  454.4 41.2 %all-reduce.4.cloned.1.call-done = f32[256,256]{0,1:T(8,128)} async-done(((f32[256,256]{0,1:T(8,128)}), f32[256,256]{0,1:T(8,128)}) %all-reduce.4.cloned.1.call-update) | async-done | bytes 262160 | tf_op jit(solution)/shard_map/psum | solution.py:34
  495.6 1.1 copy.8
  496.7 1.0 fusion.9
  497.7 11.7 %cholesky.130 = f32[128,128]{1,0:T(8,128)S(1)} custom-call(f32[128,128]{1,0:T(8,128)S(1)} %cholesky.194), custom_call_target="Cholesky" | custom-call | tf_op jit(solution)/shard_map/jit(cholesky)/cholesky | solution.py:37
  509.4 9.8 custom-call.13
  519.3 0.2 constant_dynamic-update-slice_fusion.3
  519.5 0.3 convolution_subtract_fusion.3
  519.7 11.7 %cholesky.147 = f32[128,128]{1,0:T(8,128)S(1)} custom-call(f32[128,128]{1,0:T(8,128)S(1)} %convolution_subtract_fusion.3), custom_call_target="Cholesky" | custom-call | tf_op jit(solution)/shard_map/jit(cholesky)/cholesky | solution.py:37
  531.5 0.7 compare_reduce_fusion.2
  533.6 0.1 triangular_solve.75
  533.7 4.3 while.4
  533.9 0.6 fusion.55
  534.5 1.4 bitcast_dynamic-update-slice_fusion.4
  536.0 0.6 fusion.55
  536.6 1.4 bitcast_dynamic-update-slice_fusion.4
  538.0 19.7 %custom-call.14 = f32[2,128,128]{1,2,0:T(8,128)S(1)} custom-call(f32[2,128,128]{2,1,0:T(8,128)S(1)} %get-tuple-element.18), custom_call_target="InvertDiagBlocksLowerTriangular" | custom-call | tf_op jit(solution)/shard_map/jit(_solve_triangular)/triangular_solve | solution.py:38
  557.7 3.7 fusion.3
  561.4 3.6 convolution_subtract_fusion.1
  565.0 1.9 fusion.17
  566.9 14.2 %fusion = f32[3200,256]{1,0:T(8,128)} fusion(bf16[3200,4096]{1,0:T(8,128)(2,1)} %multiply_convert_fusion, bf16[128,4096]{1,0:T(8,128)(2,1)S(1)} %fusion.17, f32[128,4096]{1,0:T(8,128)S(1)} %fusion.3), kind=kOutput, calls=%fused_computation.9 | convolution fusion | flops 6715080704 | bytes 32636928 | tf_op jit(solution)/shard_map/dot_general | solution.py:19
  581.2 45.1 %reduce-scatter.5.cloned.1.call-done = f32[800,256]{1,0:T(8,128)} async-done(((f32[3200,256]{1,0:T(8,128)}), f32[800,256]{1,0:T(8,128)}) %reduce-scatter.5.cloned.1.call-update) | async-done | bytes 819216 | tf_op jit(solution)/shard_map/reduce_scatter | solution.py:18
  626.3 2.1 multiply_convert_fusion.1
  628.4 0.0 all-gather.13.cloned.1.call-start
  628.5 31.5 %all-gather.9.cloned.1.call-done = bf16[3200,256]{1,0:T(8,128)(2,1)} async-done(((bf16[800,256]{1,0:T(8,128)(2,1)}), bf16[3200,256]{1,0:T(8,128)(2,1)}) %all-gather.9.cloned.1.call-update) | async-done | bytes 1638416 | tf_op jit(solution)/shard_map/all_gather | solution.py:28
  660.0 14.4 %fusion.32 = f32[4096,256]{1,0:T(8,128)} fusion(bf16[3200,4096]{1,0:T(8,128)(2,1)} %multiply_convert_fusion, bf16[3200,256]{1,0:T(8,128)(2,1)} %all-gather.9.cloned.1.call-done), kind=kOutput, calls=%fused_computation.68 | convolution fusion | flops 6710886400 | bytes 32047104 | tf_op jit(solution)/shard_map/dot_general | solution.py:29
  674.4 0.0 all-reduce.6.cloned.1.call-start
  674.5 288.7 %all-gather.13.cloned.1.call-done = f32[32768,256]{1,0:T(8,128)} async-done(((f32[4096,256]{1,0:T(8,128)}), f32[32768,256]{1,0:T(8,128)}) %all-gather.13.cloned.1.call-update) | async-done | bytes 33554448 | tf_op jit(solution)/shard_map/all_gather | solution.py:32
  963.2 14.5 %reduce_sum.19 = f32[4096,256]{1,0:T(8,128)} reduce(f32[8,4096,256]{2,1,0:T(8,128)} %bitcast.84, f32[]{:T(128)} %constant.69.clone.1), dimensions={0}, to_apply=%region_8.11 | reduce | flops 7340032 | bytes 37748740 | tf_op jit(solution)/shard_map/reduce_sum | solution.py:33
  977.7 10.9 fusion.33
  988.6 41.4 %all-reduce.6.cloned.1.call-done = f32[256,256]{0,1:T(8,128)} async-done(((f32[256,256]{0,1:T(8,128)}), f32[256,256]{0,1:T(8,128)}) %all-reduce.6.cloned.1.call-update) | async-done | bytes 262160 | tf_op jit(solution)/shard_map/psum | solution.py:34
  1030.0 1.1 copy.10
  1031.0 1.0 fusion.8
  1032.0 11.7 %cholesky.164 = f32[128,128]{1,0:T(8,128)S(1)} custom-call(f32[128,128]{1,0:T(8,128)S(1)} %cholesky.197), custom_call_target="Cholesky" | custom-call | tf_op jit(solution)/shard_map/jit(cholesky)/cholesky | solution.py:37
  1043.8 10.0 custom-call.15
  1053.8 0.2 constant_dynamic-update-slice_fusion.1
  1054.0 0.3 convolution_subtract_fusion.2
  1054.3 11.7 %cholesky.181 = f32[128,128]{1,0:T(8,128)S(1)} custom-call(f32[128,128]{1,0:T(8,128)S(1)} %convolution_subtract_fusion.2), custom_call_target="Cholesky" | custom-call | tf_op jit(solution)/shard_map/jit(cholesky)/cholesky | solution.py:37
  1066.1 0.7 compare_reduce_fusion
  1066.8 0.6 compare_reduce_fusion.1
  1068.7 0.7 fusion.11
  1069.5 4.1 while.5
  1069.5 0.7 fusion.56
  1070.2 1.3 bitcast_dynamic-update-slice_fusion.5
  1071.6 0.7 fusion.56
  1072.2 1.3 bitcast_dynamic-update-slice_fusion.5
  1073.6 19.9 %custom-call.16 = f32[2,128,128]{1,2,0:T(8,128)S(1)} custom-call(f32[2,128,128]{2,1,0:T(8,128)S(1)} %get-tuple-element.19), custom_call_target="InvertDiagBlocksLowerTriangular" | custom-call | tf_op jit(solution)/shard_map/jit(_solve_triangular)/triangular_solve | solution.py:38
  1093.5 3.7 fusion.1
  1097.2 3.4 convolution_subtract_fusion
  1100.7 2.0 fusion.13
  1102.7 2.4 maximum_bitcast_fusion
  1105.1 5.6 copy.11
  (35 shorter events, 0.6 us)
Async XLA Ops:
  7.2 1.1 copy-start
  7.2 84.8 %reduce-scatter.3.cloned.1.call-start = ((), (), s32[]{:S(2)}) async-start(), calls=%async_computation.2 | async-start | bytes 4096000 | tf_op jit(solution)/shard_map/reduce_scatter | solution.py:18
  44.1 81.7 %all-gather.7.cloned.1.call-start = ((), (), s32[]{:S(2)}) async-start(), calls=%async_computation.3 | async-start | bytes 2048000 | tf_op jit(solution)/shard_map/all_gather | solution.py:28
  94.0 334.9 %all-gather.11.cloned.1.call-start = ((), (), s32[]{:S(2)}) async-start(), calls=%async_computation.8 | async-start | bytes 37748736 | tf_op jit(solution)/shard_map/all_gather | solution.py:32
  140.2 355.4 %all-reduce.4.cloned.1.call-start = ((), (), s32[]{:S(2)}) async-start(), calls=%async_computation.4 | async-start | bytes 524288 | tf_op jit(solution)/shard_map/psum | solution.py:34
  454.2 172.1 %reduce-scatter.5.cloned.1.call-start = ((), (), s32[]{:S(2)}) async-start(), calls=%async_computation.5 | async-start | bytes 4096000 | tf_op jit(solution)/shard_map/reduce_scatter | solution.py:18
  557.7 3.7 copy-start.2
  581.1 78.8 %all-gather.9.cloned.1.call-start = ((), (), s32[]{:S(2)}) async-start(), calls=%async_computation.6 | async-start | bytes 2048000 | tf_op jit(solution)/shard_map/all_gather | solution.py:28
  628.4 334.8 %all-gather.13.cloned.1.call-start = ((), (), s32[]{:S(2)}) async-start(), calls=%async_computation.9 | async-start | bytes 37748736 | tf_op jit(solution)/shard_map/all_gather | solution.py:32
  674.4 355.5 %all-reduce.6.cloned.1.call-start = ((), (), s32[]{:S(2)}) async-start(), calls=%async_computation.7 | async-start | bytes 524288 | tf_op jit(solution)/shard_map/psum | solution.py:34
  1093.5 3.7 copy-start.3
  1102.6 8.0 copy-start.1
Sparse Core Ops, SparseCore 0:
  44.2 47.6 reduce-scatter.2
  94.4 31.3 all-gather.6
  140.3 288.5 all-gather.10
  454.3 41.2 all-reduce.3
  581.3 44.9 reduce-scatter.4
  628.6 31.3 all-gather.8
  674.5 288.5 all-gather.12
  988.7 41.2 all-reduce.5
